TPU v7x, 32 devices: a whole 2x2x4 slice. The times are simulated.
32 devices in a mesh: ctx: 8 (over y, x, core), fsdp: 4 (over z).
Axes of the slice: x: 2, y: 2, z: 4, core: 2. Of those that a mesh axis runs over, the one named last changes fastest.
Arguments:
- tokens_in: bfloat16 [4, 1024, 1024], P('fsdp', 'ctx'), may hold values from -6 to 6
- doc_lengths: int32 [4, 8], P('fsdp'), may hold values from 1 to 512, 1024 in all within a row
- norm1_gain: bfloat16 [1024], P('fsdp'), may hold values from 0.5 to 1.5
- norm1_bias: bfloat16 [1024], P('fsdp'), may hold values from -1.5 to 1.5
- qkv_weight: bfloat16 [1024, 3072], P('fsdp'), may hold values from -0.1875 to 0.1875
- qv_bias: bfloat16 [2048], P('fsdp'), may hold values from -1.5 to 1.5
- out_weight: bfloat16 [1024, 1024], P('fsdp'), may hold values from -1.5 to 1.5
- out_bias: bfloat16 [1024], P('fsdp'), may hold values from -1.5 to 1.5
- norm2_gain: bfloat16 [1024], P('fsdp'), may hold values from 0.5 to 1.5
- norm2_bias: bfloat16 [1024], P('fsdp'), may hold values from -1.5 to 1.5
- up_weight: bfloat16 [1024, 4096], P('fsdp'), may hold values from -0.1875 to 0.1875
- up_bias: bfloat16 [4096], P('fsdp'), may hold values from -1.5 to 1.5
- down_weight: bfloat16 [4096, 1024], P('fsdp'), may hold values from -0.09375 to 0.09375
- down_bias: bfloat16 [1024], P('fsdp'), may hold values from -1.5 to 1.5
- out_cotangent: bfloat16 [4, 1024, 1024], P('fsdp', 'ctx'), may hold values from -6 to 6
Outputs:
- layer_out: bfloat16 [4, 1024, 1024], P('fsdp', 'ctx')
- input_grad: bfloat16 [4, 1024, 1024], P('fsdp', 'ctx')
- norm1_gain_grad: float32 [1024], P(('ctx', 'fsdp'))
- norm1_bias_grad: float32 [1024], P(('ctx', 'fsdp'))
- qkv_weight_grad: float32 [1024, 3072], P(('ctx', 'fsdp'))
- qv_bias_grad: float32 [2048], P(('ctx', 'fsdp'))
- out_weight_grad: float32 [1024, 1024], P(('ctx', 'fsdp'))
- out_bias_grad: float32 [1024], P(('ctx', 'fsdp'))
- norm2_gain_grad: float32 [1024], P(('ctx', 'fsdp'))
- norm2_bias_grad: float32 [1024], P(('ctx', 'fsdp'))
- up_weight_grad: float32 [1024, 4096], P(('ctx', 'fsdp'))
- up_bias_grad: float32 [4096], P(('ctx', 'fsdp'))
- down_weight_grad: float32 [4096, 1024], P(('ctx', 'fsdp'))
- down_bias_grad: float32 [1024], P(('ctx', 'fsdp'))
Inputs may be any that keep to these rules, and one draw needn't show every extreme that they name: `doc_lengths`: each row lists one stream's documents in order; they sum to 1024; the longest is 512.
All inputs are finite; a program needn't handle non-finite values.
Results may differ from a plain program's by a relative error of at most 0.018.
Values may be sent and summed in bfloat16 or wider, within the bound.
A program may use at most 128 MiB of HBM per device.

v0:
```python
import jax
import jax.numpy as jnp
from jax import lax
from jax.sharding import PartitionSpec as P

HEADS = 16
HEAD_DIM = 64
epsilon = 1e-05
masked_score = -1e30


def passed_along(block, axis, distance):
    devices = range(lax.axis_size(axis))
    route = [(i - distance, i) for i in devices if i - distance in devices]
    return lax.ppermute(block, axis, route)


def from_behind(x, axis, by):
    size = lax.axis_size(axis)
    return lax.ppermute(x, axis, [(i, (i + by) % size) for i in range(size)])


def norm_rows(values, gain, offset):
    centre = values - jnp.mean(values, axis=-1, keepdims=True)
    spread = jnp.mean(centre * centre, axis=-1, keepdims=True)
    return centre * lax.rsqrt(spread + epsilon) * gain + offset


def gelu_tanh(values):
    return jax.nn.gelu(values, approximate=True)


def doc_index(positions, doc_ends):
    return jnp.sum((doc_ends[None, :] <= positions[:, None]).astype(jnp.int32), axis=1)


def shards(
    tokens_in,
    doc_lengths,
    norm1_gain,
    norm1_bias,
    qkv_weight,
    qv_bias,
    out_weight,
    out_bias,
    norm2_gain,
    norm2_bias,
    up_weight,
    up_bias,
    down_weight,
    down_bias,
    out_cotangent,
):
    model_width = tokens_in.shape[2]
    tok_rows = tokens_in.shape[1]
    ctx_count = lax.axis_size("ctx")
    ctx_index = lax.axis_index("ctx")
    score_scale = HEAD_DIM ** (-0.5)
    inputs = tokens_in[0].astype(jnp.float32)
    doc_ends = jnp.cumsum(doc_lengths[0])
    query_pos = ctx_index * tok_rows + jnp.arange(tok_rows, dtype=jnp.int32)
    query_doc = doc_index(query_pos, doc_ends)

    def block_mask(anchor):
        key_pos = anchor * tok_rows + jnp.arange(tok_rows, dtype=jnp.int32)
        key_doc = doc_index(key_pos, doc_ends)
        return (key_pos[None, :] <= query_pos[:, None]) & (key_doc[None, :] == query_doc[:, None])

    attn_set = (
        lax.all_gather(norm1_gain, "fsdp", axis=0, tiled=True),
        lax.all_gather(norm1_bias, "fsdp", axis=0, tiled=True),
        lax.all_gather(qkv_weight, "fsdp", axis=0, tiled=True),
        lax.all_gather(qv_bias, "fsdp", axis=0, tiled=True),
        lax.all_gather(out_weight, "fsdp", axis=0, tiled=True),
        lax.all_gather(out_bias, "fsdp", axis=0, tiled=True),
    )
    gain_one, shift_one, w_qkv, b_qv, w_out, b_out = attn_set
    gain_one_f = gain_one.astype(jnp.float32)
    shift_one_f = shift_one.astype(jnp.float32)
    normed1 = norm_rows(inputs, gain_one_f, shift_one_f).astype(jnp.bfloat16)
    bias_full = jnp.concatenate(
        [b_qv[:model_width], jnp.zeros((model_width,), b_qv.dtype), b_qv[model_width:]]
    ).astype(jnp.float32)
    projected = (jnp.dot(normed1, w_qkv, preferred_element_type=jnp.float32) + bias_full).astype(
        jnp.bfloat16
    )
    queries = projected[:, :model_width].reshape(tok_rows, HEADS, HEAD_DIM)
    keys_own = projected[:, model_width : 2 * model_width].reshape(tok_rows, HEADS, HEAD_DIM)
    values_own = projected[:, 2 * model_width :].reshape(tok_rows, HEADS, HEAD_DIM)

    def attend(carry, keys, values, anchor):
        accum, running_top, running_total = carry
        allowed = block_mask(anchor)
        scores = (
            jnp.einsum("thd,shd->hts", queries, keys, preferred_element_type=jnp.float32)
            * score_scale
        )
        scores = jnp.where(allowed[None], scores, masked_score)
        new_top = jnp.maximum(running_top, jnp.max(scores, axis=2))
        weights = jnp.exp(scores - new_top[:, :, None])
        factor = jnp.exp(running_top - new_top)
        running_total = running_total * factor + jnp.sum(weights, axis=2)
        block_part = jnp.einsum(
            "hts,shd->thd", weights.astype(jnp.bfloat16), values, preferred_element_type=jnp.float32
        )
        accum = accum * factor.T[:, :, None] + block_part
        return (accum, new_top, running_total)

    start_carry = (
        jnp.zeros((tok_rows, HEADS, HEAD_DIM), jnp.float32),
        jnp.full((HEADS, tok_rows), masked_score, jnp.float32),
        jnp.zeros((HEADS, tok_rows), jnp.float32),
    )
    first_carry = attend(start_carry, keys_own, values_own, ctx_index)

    def cycle_forward(cycle_step, state):
        keys, values, carry = state
        keys, values = passed_along((keys, values), "ctx", 1)
        anchor = (ctx_index - cycle_step) % ctx_count
        return (keys, values, attend(carry, keys, values, anchor))

    _, _, final_carry = lax.fori_loop(
        1, ctx_count, cycle_forward, (keys_own, values_own, first_carry)
    )
    accum, running_top, running_total = final_carry
    log_total = running_top + jnp.log(running_total)
    mix = (accum / running_total.T[:, :, None]).reshape(tok_rows, model_width).astype(jnp.bfloat16)
    resid = (
        inputs + jnp.dot(mix, w_out, preferred_element_type=jnp.float32) + b_out.astype(jnp.float32)
    )
    mlp_set = (
        lax.all_gather(norm2_gain, "fsdp", axis=0, tiled=True),
        lax.all_gather(norm2_bias, "fsdp", axis=0, tiled=True),
        lax.all_gather(up_weight, "fsdp", axis=0, tiled=True),
        lax.all_gather(up_bias, "fsdp", axis=0, tiled=True),
        lax.all_gather(down_weight, "fsdp", axis=0, tiled=True),
        lax.all_gather(down_bias, "fsdp", axis=0, tiled=True),
    )
    gain_two, shift_two, w_up, b_up, w_down, b_down = mlp_set
    gain_two_f = gain_two.astype(jnp.float32)
    shift_two_f = shift_two.astype(jnp.float32)
    normed2 = norm_rows(resid, gain_two_f, shift_two_f).astype(jnp.bfloat16)
    pre = jnp.dot(normed2, w_up, preferred_element_type=jnp.float32) + b_up.astype(jnp.float32)
    hidden = gelu_tanh(pre).astype(jnp.bfloat16)
    result = (
        resid
        + jnp.dot(hidden, w_down, preferred_element_type=jnp.float32)
        + b_down.astype(jnp.float32)
    )
    layer_out = result.astype(jnp.bfloat16)[None]
    cotangent = out_cotangent[0]
    cotangent_f = cotangent.astype(jnp.float32)
    down_w_grad = jnp.einsum("tf,td->fd", hidden, cotangent, preferred_element_type=jnp.float32)
    down_b_grad = jnp.sum(cotangent_f, axis=0)
    hidden_grad = jnp.einsum("td,fd->tf", cotangent, w_down, preferred_element_type=jnp.float32)
    _, gelu_pull = jax.vjp(gelu_tanh, pre)
    pre_grad = gelu_pull(hidden_grad)[0].astype(jnp.bfloat16)
    up_w_grad = jnp.einsum("td,tf->df", normed2, pre_grad, preferred_element_type=jnp.float32)
    up_b_grad = jnp.sum(pre_grad.astype(jnp.float32), axis=0)
    normed2_grad = jnp.einsum("tf,df->td", pre_grad, w_up, preferred_element_type=jnp.float32)
    _, norm_two_pull = jax.vjp(norm_rows, resid, gain_two_f, shift_two_f)
    resid_part, gain_two_grad, shift_two_grad = norm_two_pull(normed2_grad)
    resid_grad = cotangent_f + resid_part
    mlp_sums = (
        lax.psum_scatter(gain_two_grad, ("ctx", "fsdp"), scatter_dimension=0, tiled=True),
        lax.psum_scatter(shift_two_grad, ("ctx", "fsdp"), scatter_dimension=0, tiled=True),
        lax.psum_scatter(up_w_grad, ("ctx", "fsdp"), scatter_dimension=0, tiled=True),
        lax.psum_scatter(up_b_grad, ("ctx", "fsdp"), scatter_dimension=0, tiled=True),
        lax.psum_scatter(down_w_grad, ("ctx", "fsdp"), scatter_dimension=0, tiled=True),
        lax.psum_scatter(down_b_grad, ("ctx", "fsdp"), scatter_dimension=0, tiled=True),
    )
    branch_grad = resid_grad.astype(jnp.bfloat16)
    out_w_grad = jnp.einsum("td,te->de", mix, branch_grad, preferred_element_type=jnp.float32)
    out_b_grad = jnp.sum(branch_grad.astype(jnp.float32), axis=0)
    mix_grad = jnp.einsum(
        "te,de->td", branch_grad, w_out, preferred_element_type=jnp.float32
    ).astype(jnp.bfloat16)
    mix_grad = mix_grad.reshape(tok_rows, HEADS, HEAD_DIM)
    delta = jnp.sum(
        mix_grad.astype(jnp.float32) * mix.reshape(tok_rows, HEADS, HEAD_DIM).astype(jnp.float32),
        axis=2,
    ).T

    def attend_back(query_grad, keys, values, key_grads, value_grads, anchor):
        allowed = block_mask(anchor)
        scores = (
            jnp.einsum("thd,shd->hts", queries, keys, preferred_element_type=jnp.float32)
            * score_scale
        )
        probs = jnp.where(allowed[None], jnp.exp(scores - log_total[:, :, None]), 0.0)
        value_grads = value_grads + jnp.einsum(
            "hts,thd->shd", probs.astype(jnp.bfloat16), mix_grad, preferred_element_type=jnp.float32
        )
        prob_grads = jnp.einsum(
            "thd,shd->hts", mix_grad, values, preferred_element_type=jnp.float32
        )
        score_grads = (probs * (prob_grads - delta[:, :, None])).astype(jnp.bfloat16)
        query_grad = query_grad + score_scale * jnp.einsum(
            "hts,shd->thd", score_grads, keys, preferred_element_type=jnp.float32
        )
        key_grads = key_grads + score_scale * jnp.einsum(
            "hts,thd->shd", score_grads, queries, preferred_element_type=jnp.float32
        )
        return (query_grad, key_grads, value_grads)

    def cycle_backward(cycle_step, state):
        keys, values, key_grads, value_grads, query_grad = state
        anchor = (ctx_index - cycle_step) % ctx_count
        query_grad, key_grads, value_grads = attend_back(
            query_grad, keys, values, key_grads, value_grads, anchor
        )
        keys, values, key_grads, value_grads = (
            from_behind(keys, "ctx", 1),
            from_behind(values, "ctx", 1),
            from_behind(key_grads.astype(jnp.bfloat16), "ctx", 1).astype(key_grads.dtype),
            from_behind(value_grads.astype(jnp.bfloat16), "ctx", 1).astype(value_grads.dtype),
        )
        return (keys, values, key_grads, value_grads, query_grad)

    zero_grads = jnp.zeros((tok_rows, HEADS, HEAD_DIM), jnp.float32)
    back_state = lax.fori_loop(
        0, ctx_count, cycle_backward, (keys_own, values_own, zero_grads, zero_grads, zero_grads)
    )
    key_grads = back_state[2]
    value_grads = back_state[3]
    query_grad = back_state[4]
    qkv_grad = jnp.concatenate(
        [
            query_grad.reshape(tok_rows, model_width),
            key_grads.reshape(tok_rows, model_width),
            value_grads.reshape(tok_rows, model_width),
        ],
        axis=1,
    ).astype(jnp.bfloat16)
    qkv_w_grad = jnp.einsum("td,te->de", normed1, qkv_grad, preferred_element_type=jnp.float32)
    column_sums = jnp.sum(qkv_grad.astype(jnp.float32), axis=0)
    qv_b_grad = jnp.concatenate([column_sums[:model_width], column_sums[2 * model_width :]])
    normed1_grad = jnp.einsum("te,de->td", qkv_grad, w_qkv, preferred_element_type=jnp.float32)
    _, norm_one_pull = jax.vjp(norm_rows, inputs, gain_one_f, shift_one_f)
    input_part, gain_one_grad, shift_one_grad = norm_one_pull(normed1_grad)
    input_grad = (resid_grad + input_part).astype(jnp.bfloat16)[None]
    attn_sums = (
        lax.psum_scatter(gain_one_grad, ("ctx", "fsdp"), scatter_dimension=0, tiled=True),
        lax.psum_scatter(shift_one_grad, ("ctx", "fsdp"), scatter_dimension=0, tiled=True),
        lax.psum_scatter(qkv_w_grad, ("ctx", "fsdp"), scatter_dimension=0, tiled=True),
        lax.psum_scatter(qv_b_grad, ("ctx", "fsdp"), scatter_dimension=0, tiled=True),
        lax.psum_scatter(out_w_grad, ("ctx", "fsdp"), scatter_dimension=0, tiled=True),
        lax.psum_scatter(out_b_grad, ("ctx", "fsdp"), scatter_dimension=0, tiled=True),
    )
    return (
        layer_out,
        input_grad,
        attn_sums[0],
        attn_sums[1],
        attn_sums[2],
        attn_sums[3],
        attn_sums[4],
        attn_sums[5],
        mlp_sums[0],
        mlp_sums[1],
        mlp_sums[2],
        mlp_sums[3],
        mlp_sums[4],
        mlp_sums[5],
    )


def solution(mesh):
    placed = (
        P("fsdp", "ctx", None),
        P("fsdp", None),
        P("fsdp"),
        P("fsdp"),
        P("fsdp", None),
        P("fsdp"),
        P("fsdp", None),
        P("fsdp"),
        P("fsdp"),
        P("fsdp"),
        P("fsdp", None),
        P("fsdp"),
        P("fsdp", None),
        P("fsdp"),
        P("fsdp", "ctx", None),
    )
    return jax.shard_map(
        shards,
        mesh=mesh,
        in_specs=placed,
        out_specs=(
            P("fsdp", "ctx", None),
            P("fsdp", "ctx", None),
            P(("ctx", "fsdp")),
            P(("ctx", "fsdp")),
            P(("ctx", "fsdp"), None),
            P(("ctx", "fsdp")),
            P(("ctx", "fsdp"), None),
            P(("ctx", "fsdp")),
            P(("ctx", "fsdp")),
            P(("ctx", "fsdp")),
            P(("ctx", "fsdp"), None),
            P(("ctx", "fsdp")),
            P(("ctx", "fsdp"), None),
            P(("ctx", "fsdp")),
        ),
        check_vma=False,
    )
```

profile of v0, /device:TPU:0, one launch (start us, length us, event | category | flops | bytes accessed | tf_op | source)
XLA Modules:
  0.0 1537.0 jit_solution(3058902817003224563)
XLA Ops:
  10.2 12.6 all-gather.3
  22.8 13.5 all-gather.2
  36.3 8.5 all-gather.1
  44.8 14.5 all-gather
  60.2 12.0 all_gather.45
  72.2 7.7 all-gather.5
  80.0 13.6 all-gather.4
  93.6 34.6 %all-gather.12.cloned.1.call-done = bf16[1024,3072]{1,0:T(8,128)(2,1)} async-done(((bf16[256,3072]{1,0:T(8,128)(2,1)}), bf16[1024,3072]{1,0:T(8,128)(2,1)}) %all-gather.12.cloned.1.call-update) | async-done | bytes 6291472 | tf_op jit(solution)/shard_map/all_gather | solution.py:72
  136.8 79.3 %while.48 = (s32[]{:T(128)}, bf16[128,16,64]{0,2,1:T(8,128)(2,1)S(1)}, bf16[128,16,64]{0,2,1:T(8,128)(2,1)}, f32[128,16,64]{0,2,1:T(8,128)S(1)}, f32[16,128]{1,0...) while((s32[]{:T(128)}, ...), condition=%wide.region_10.11_spmd.clone, body=%wide.region_6.0_spmd.clone.sunk | while | flops 69264528 | bytes 8294802 | solution.py:122
  191.2 5.8 collective-permute-start
  218.6 105.3 %all-gather.16.cloned.1.call-done = bf16[1024,4096]{1,0:T(8,128)(2,1)} async-done(((bf16[256,4096]{1,0:T(8,128)(2,1)}), bf16[1024,4096]{1,0:T(8,128)(2,1)}) %all-gather.16.cloned.1.call-update) | async-done | bytes 8388624 | tf_op jit(solution)/shard_map/all_gather | solution.py:134
  323.8 6.1 convolution_add_fusion
  329.9 143.2 %all-gather.18.cloned.1.call-done = bf16[4096,1024]{1,0:T(8,128)(2,1)} async-done(((bf16[1024,1024]{1,0:T(8,128)(2,1)}), bf16[4096,1024]{1,0:T(8,128)(2,1)}) %all-gather.18.cloned.1.call-update) | async-done | bytes 8388624 | tf_op jit(solution)/shard_map/all_gather | solution.py:136
  473.2 7.8 convert_reduce_fusion.2
  490.8 145.1 %while.49 = (s32[]{:T(128)}, bf16[128,16,64]{0,2,1:T(8,128)(2,1)S(1)}, bf16[128,16,64]{0,2,1:T(8,128)(2,1)}, f32[128,16,64]{0,2,1:T(8,128)S(1)}, f32[128,16,64]{...) while((s32[]{:T(128)}, ...), condition=%wide.region_18.19_spmd.clone, body=%wide.region_16.18_spmd.clone.sunk | while | flops 171232400 | bytes 16044550 | solution.py:221
  637.1 6.4 fusion.66
  644.8 9.0 fusion.71
  654.8 10.7 fusion.56
  666.2 9.3 all-gather.6
  682.7 43.7 %all-reduce.8 = (f32[1024]{0:T(1024)S(1)}, f32[1024]{0:T(1024)S(1)}, f32[2048]{0:T(1024)S(1)}, f32[1024]{0:T(1024)S(1)}, f32[1024]{0:T(1024)S(1)}, /*index=5*/f3...) all-reduce(f32[1024]{0:T(1024)S(1)} %get-tuple-element.720, ...), channel_id=2, replica_groups=mesh['ctx'=8,'fsdp'=4] {'ctx','fsdp'}, use_global_device_ids=true, to_apply=%region_22.23.clone | all-reduce | flops 12288 | bytes 98304
  731.1 6.5 fusion.37
  737.7 61.1 %reduce-scatter.5.cloned.1.call-done = f32[32,3072]{1,0:T(8,128)} async-done(((f32[1024,3072]{1,0:T(8,128)}), f32[32,3072]{1,0:T(8,128)}) %reduce-scatter.5.cloned.1.call-update) | async-done | bytes 393232 | tf_op jit(solution)/shard_map/reduce_scatter | solution.py:245
  798.7 366.3 %reduce-scatter.9.cloned.1.call-done = f32[32,4096]{1,0:T(8,128)} async-done(((f32[1024,4096]{1,0:T(8,128)}), f32[32,4096]{1,0:T(8,128)}) %reduce-scatter.9.cloned.1.call-update) | async-done | bytes 524304 | tf_op jit(solution)/shard_map/reduce_scatter | solution.py:167
  1165.0 365.1 %reduce-scatter.11.cloned.1.call-done = f32[128,1024]{1,0:T(8,128)} async-done(((f32[4096,1024]{1,0:T(8,128)}), f32[128,1024]{1,0:T(8,128)}) %reduce-scatter.11.cloned.1.call-update) | async-done | bytes 524304 | tf_op jit(solution)/shard_map/reduce_scatter | solution.py:169
  (409 shorter events, 257.0 us)
Async XLA Ops:
  7.2 121.0 %all-gather.12.cloned.1.call-start = ((), (), s32[]{:S(2)}) async-start(), calls=%async_computation.4 | async-start | bytes 7864320 | tf_op jit(solution)/shard_map/all_gather | solution.py:72
  7.9 208.3 %all-gather.14.cloned.1.call-start = ((), (), s32[]{:S(2)}) async-start(), calls=%async_computation.5 | async-start | bytes 2621440 | tf_op jit(solution)/shard_map/all_gather | solution.py:74
  8.8 315.1 %all-gather.16.cloned.1.call-start = ((), (), s32[]{:S(2)}) async-start(), calls=%async_computation.6 | async-start | bytes 10485760 | tf_op jit(solution)/shard_map/all_gather | solution.py:134
  9.5 463.7 %all-gather.18.cloned.1.call-start = ((), (), s32[]{:S(2)}) async-start(), calls=%async_computation.7 | async-start | bytes 10485760 | tf_op jit(solution)/shard_map/all_gather | solution.py:136
  10.1 727.6 %reduce-scatter.7.cloned.1.call-start = ((), (), s32[]{:S(2)}) async-start(), calls=%async_computation.9 | async-start | bytes 4325376 | tf_op jit(solution)/shard_map/reduce_scatter | solution.py:247
  490.8 308.0 %reduce-scatter.5.cloned.1.call-start = ((), (), s32[]{:S(2)}) async-start(), calls=%async_computation.8 | async-start | bytes 12976128 | tf_op jit(solution)/shard_map/reduce_scatter | solution.py:245
  491.1 17.7 %collective-permute-start.2 = (bf16[128,16,64]{0,2,1:T(8,128)(2,1)S(1)}, bf16[128,16,64]{0,2,1:T(8,128)(2,1)S(1)}, u32[]{:S(2)}, u32[]{:S(2)}) collective-permute-start(bf16[128,16,64]{0,2,1:T(8,128)(2,1)S(1)} %copy.89), channel_id=1, source_target_pairs={{0,4},{4,8},{8,12},{12,16},{16,20},{20,24},{24,28},{28,0},{1,5},{5... | collective-permute-start | bytes 786440 | tf_op jit(solution)/shard_map/while/body/eval_jaxpr/ppermute | solution.py:20
  492.1 16.6 %collective-permute-start.3 = (bf16[128,16,64]{0,2,1:T(8,128)(2,1)S(1)}, bf16[128,16,64]{0,2,1:T(8,128)(2,1)}, u32[]{:S(2)}, u32[]{:S(2)}) collective-permute-start(bf16[128,16,64]{0,2,1:T(8,128)(2,1)S(1)} %copy.90), channel_id=1, source_target_pairs={{0,4},{4,8},{8,12},{12,16},{16,20},{20,24},{24,28},{28,0},{1,5},{5... | collective-permute-start | bytes 786440 | tf_op jit(solution)/shard_map/while/body/eval_jaxpr/ppermute | solution.py:20
  508.8 18.3 %collective-permute-start.2 = (bf16[128,16,64]{0,2,1:T(8,128)(2,1)S(1)}, bf16[128,16,64]{0,2,1:T(8,128)(2,1)S(1)}, u32[]{:S(2)}, u32[]{:S(2)}) collective-permute-start(bf16[128,16,64]{0,2,1:T(8,128)(2,1)S(1)} %copy.89), channel_id=1, source_target_pairs={{0,4},{4,8},{8,12},{12,16},{16,20},{20,24},{24,28},{28,0},{1,5},{5... | collective-permute-start | bytes 786440 | tf_op jit(solution)/shard_map/while/body/eval_jaxpr/ppermute | solution.py:20
  509.8 17.3 %collective-permute-start.3 = (bf16[128,16,64]{0,2,1:T(8,128)(2,1)S(1)}, bf16[128,16,64]{0,2,1:T(8,128)(2,1)}, u32[]{:S(2)}, u32[]{:S(2)}) collective-permute-start(bf16[128,16,64]{0,2,1:T(8,128)(2,1)S(1)} %copy.90), channel_id=1, source_target_pairs={{0,4},{4,8},{8,12},{12,16},{16,20},{20,24},{24,28},{28,0},{1,5},{5... | collective-permute-start | bytes 786440 | tf_op jit(solution)/shard_map/while/body/eval_jaxpr/ppermute | solution.py:20
  527.2 18.2 %collective-permute-start.2 = (bf16[128,16,64]{0,2,1:T(8,128)(2,1)S(1)}, bf16[128,16,64]{0,2,1:T(8,128)(2,1)S(1)}, u32[]{:S(2)}, u32[]{:S(2)}) collective-permute-start(bf16[128,16,64]{0,2,1:T(8,128)(2,1)S(1)} %copy.89), channel_id=1, source_target_pairs={{0,4},{4,8},{8,12},{12,16},{16,20},{20,24},{24,28},{28,0},{1,5},{5... | collective-permute-start | bytes 786440 | tf_op jit(solution)/shard_map/while/body/eval_jaxpr/ppermute | solution.py:20
  528.2 17.2 %collective-permute-start.3 = (bf16[128,16,64]{0,2,1:T(8,128)(2,1)S(1)}, bf16[128,16,64]{0,2,1:T(8,128)(2,1)}, u32[]{:S(2)}, u32[]{:S(2)}) collective-permute-start(bf16[128,16,64]{0,2,1:T(8,128)(2,1)S(1)} %copy.90), channel_id=1, source_target_pairs={{0,4},{4,8},{8,12},{12,16},{16,20},{20,24},{24,28},{28,0},{1,5},{5... | collective-permute-start | bytes 786440 | tf_op jit(solution)/shard_map/while/body/eval_jaxpr/ppermute | solution.py:20
  545.4 18.1 %collective-permute-start.2 = (bf16[128,16,64]{0,2,1:T(8,128)(2,1)S(1)}, bf16[128,16,64]{0,2,1:T(8,128)(2,1)S(1)}, u32[]{:S(2)}, u32[]{:S(2)}) collective-permute-start(bf16[128,16,64]{0,2,1:T(8,128)(2,1)S(1)} %copy.89), channel_id=1, source_target_pairs={{0,4},{4,8},{8,12},{12,16},{16,20},{20,24},{24,28},{28,0},{1,5},{5... | collective-permute-start | bytes 786440 | tf_op jit(solution)/shard_map/while/body/eval_jaxpr/ppermute | solution.py:20
  546.5 17.1 %collective-permute-start.3 = (bf16[128,16,64]{0,2,1:T(8,128)(2,1)S(1)}, bf16[128,16,64]{0,2,1:T(8,128)(2,1)}, u32[]{:S(2)}, u32[]{:S(2)}) collective-permute-start(bf16[128,16,64]{0,2,1:T(8,128)(2,1)S(1)} %copy.90), channel_id=1, source_target_pairs={{0,4},{4,8},{8,12},{12,16},{16,20},{20,24},{24,28},{28,0},{1,5},{5... | collective-permute-start | bytes 786440 | tf_op jit(solution)/shard_map/while/body/eval_jaxpr/ppermute | solution.py:20
  563.6 18.0 %collective-permute-start.2 = (bf16[128,16,64]{0,2,1:T(8,128)(2,1)S(1)}, bf16[128,16,64]{0,2,1:T(8,128)(2,1)S(1)}, u32[]{:S(2)}, u32[]{:S(2)}) collective-permute-start(bf16[128,16,64]{0,2,1:T(8,128)(2,1)S(1)} %copy.89), channel_id=1, source_target_pairs={{0,4},{4,8},{8,12},{12,16},{16,20},{20,24},{24,28},{28,0},{1,5},{5... | collective-permute-start | bytes 786440 | tf_op jit(solution)/shard_map/while/body/eval_jaxpr/ppermute | solution.py:20
  564.6 17.0 %collective-permute-start.3 = (bf16[128,16,64]{0,2,1:T(8,128)(2,1)S(1)}, bf16[128,16,64]{0,2,1:T(8,128)(2,1)}, u32[]{:S(2)}, u32[]{:S(2)}) collective-permute-start(bf16[128,16,64]{0,2,1:T(8,128)(2,1)S(1)} %copy.90), channel_id=1, source_target_pairs={{0,4},{4,8},{8,12},{12,16},{16,20},{20,24},{24,28},{28,0},{1,5},{5... | collective-permute-start | bytes 786440 | tf_op jit(solution)/shard_map/while/body/eval_jaxpr/ppermute | solution.py:20
  581.7 18.0 %collective-permute-start.2 = (bf16[128,16,64]{0,2,1:T(8,128)(2,1)S(1)}, bf16[128,16,64]{0,2,1:T(8,128)(2,1)S(1)}, u32[]{:S(2)}, u32[]{:S(2)}) collective-permute-start(bf16[128,16,64]{0,2,1:T(8,128)(2,1)S(1)} %copy.89), channel_id=1, source_target_pairs={{0,4},{4,8},{8,12},{12,16},{16,20},{20,24},{24,28},{28,0},{1,5},{5... | collective-permute-start | bytes 786440 | tf_op jit(solution)/shard_map/while/body/eval_jaxpr/ppermute | solution.py:20
  582.7 17.0 %collective-permute-start.3 = (bf16[128,16,64]{0,2,1:T(8,128)(2,1)S(1)}, bf16[128,16,64]{0,2,1:T(8,128)(2,1)}, u32[]{:S(2)}, u32[]{:S(2)}) collective-permute-start(bf16[128,16,64]{0,2,1:T(8,128)(2,1)S(1)} %copy.90), channel_id=1, source_target_pairs={{0,4},{4,8},{8,12},{12,16},{16,20},{20,24},{24,28},{28,0},{1,5},{5... | collective-permute-start | bytes 786440 | tf_op jit(solution)/shard_map/while/body/eval_jaxpr/ppermute | solution.py:20
  599.8 18.0 %collective-permute-start.2 = (bf16[128,16,64]{0,2,1:T(8,128)(2,1)S(1)}, bf16[128,16,64]{0,2,1:T(8,128)(2,1)S(1)}, u32[]{:S(2)}, u32[]{:S(2)}) collective-permute-start(bf16[128,16,64]{0,2,1:T(8,128)(2,1)S(1)} %copy.89), channel_id=1, source_target_pairs={{0,4},{4,8},{8,12},{12,16},{16,20},{20,24},{24,28},{28,0},{1,5},{5... | collective-permute-start | bytes 786440 | tf_op jit(solution)/shard_map/while/body/eval_jaxpr/ppermute | solution.py:20
  600.8 17.0 %collective-permute-start.3 = (bf16[128,16,64]{0,2,1:T(8,128)(2,1)S(1)}, bf16[128,16,64]{0,2,1:T(8,128)(2,1)}, u32[]{:S(2)}, u32[]{:S(2)}) collective-permute-start(bf16[128,16,64]{0,2,1:T(8,128)(2,1)S(1)} %copy.90), channel_id=1, source_target_pairs={{0,4},{4,8},{8,12},{12,16},{16,20},{20,24},{24,28},{28,0},{1,5},{5... | collective-permute-start | bytes 786440 | tf_op jit(solution)/shard_map/while/body/eval_jaxpr/ppermute | solution.py:20
  617.9 18.0 %collective-permute-start.2 = (bf16[128,16,64]{0,2,1:T(8,128)(2,1)S(1)}, bf16[128,16,64]{0,2,1:T(8,128)(2,1)S(1)}, u32[]{:S(2)}, u32[]{:S(2)}) collective-permute-start(bf16[128,16,64]{0,2,1:T(8,128)(2,1)S(1)} %copy.89), channel_id=1, source_target_pairs={{0,4},{4,8},{8,12},{12,16},{16,20},{20,24},{24,28},{28,0},{1,5},{5... | collective-permute-start | bytes 786440 | tf_op jit(solution)/shard_map/while/body/eval_jaxpr/ppermute | solution.py:20
  618.9 17.0 %collective-permute-start.3 = (bf16[128,16,64]{0,2,1:T(8,128)(2,1)S(1)}, bf16[128,16,64]{0,2,1:T(8,128)(2,1)}, u32[]{:S(2)}, u32[]{:S(2)}) collective-permute-start(bf16[128,16,64]{0,2,1:T(8,128)(2,1)S(1)} %copy.90), channel_id=1, source_target_pairs={{0,4},{4,8},{8,12},{12,16},{16,20},{20,24},{24,28},{28,0},{1,5},{5... | collective-permute-start | bytes 786440 | tf_op jit(solution)/shard_map/while/body/eval_jaxpr/ppermute | solution.py:20
  643.6 521.4 %reduce-scatter.9.cloned.1.call-start = ((), (), s32[]{:S(2)}) async-start(), calls=%async_computation.10 | async-start | bytes 17301504 | tf_op jit(solution)/shard_map/reduce_scatter | solution.py:167
  653.8 876.3 %reduce-scatter.11.cloned.1.call-start = ((), (), s32[]{:S(2)}) async-start(), calls=%async_computation.11 | async-start | bytes 17301504 | tf_op jit(solution)/shard_map/reduce_scatter | solution.py:169
  (48 other events, 823.2 us)
Sparse Core Ops, SparseCore 0:
  9.6 118.5 all-gather.11
  129.7 44.0 all-gather.13
  175.5 148.3 all-gather.15
  325.3 147.8 all-gather.17
  490.9 145.9 reduce-scatter.6
  643.7 154.9 reduce-scatter.4
  801.7 363.2 reduce-scatter.8
  1168.0 362.1 reduce-scatter.10
where the time goes:
time: 1540 us
  waiting for transfers between devices  1130 us (73%)
  blocking collectives  135 us (9%)
  matrix products  114 us (7%)
  starting transfers between devices  90.4 us (6%)
  other arithmetic  24.6 us (2%)
  local copies, waits for them, and re-layouts  24.2 us (2%)
    reduce_scatter x1, waiting for transfers between devices, shards(): lax.psum_scatter(up_w_grad, ('ctx', 'fsdp'), scatter_dimension=0, tiled=T...  366 us
    reduce_scatter x1, waiting for transfers between devices, shards(): lax.psum_scatter(down_w_grad, ('ctx', 'fsdp'), scatter_dimension=0, tiled...  365 us
    all_gather x1, waiting for transfers between devices, shards(): lax.all_gather(down_weight, 'fsdp', axis=0, tiled=True)  143 us
    all_gather x1, waiting for transfers between devices, shards(): lax.all_gather(up_weight, 'fsdp', axis=0, tiled=True)  105 us
    ppermute x14, starting transfers between devices, passed_along(): return lax.ppermute(block, axis, route)  62.4 us
    reduce_scatter x1, waiting for transfers between devices, shards(): lax.psum_scatter(qkv_w_grad, ('ctx', 'fsdp'), scatter_dimension=0, tiled=...  61.1 us
    ppermute x32, waiting for transfers between devices, from_behind(): return lax.ppermute(x, axis, [(i, (i + by) % size) for i in range(size)])  50 us
    unnamed x1, blocking collectives  43.7 us
  transfers between devices with their start and end apart: 54, of which 29 were waited for; matrix products, arithmetic and copies ran while one was open for 9% of the time, Pallas kernels for 0%

commit v1 on v0

--- a/solution.py
+++ b/solution.py
@@ -7,6 +7,23 @@
 HEAD_DIM = 64
 epsilon = 1e-05
 masked_score = -1e30
+
+
+def laid_out(blocks, dim):
+    blocks = jnp.moveaxis(blocks, 0, dim)
+    shape = blocks.shape
+    return blocks.reshape(*shape[:dim], shape[dim] * shape[dim + 1], *shape[dim + 2 :])
+
+
+def ring_gather(shard, axis, dim):
+    size = lax.axis_size(axis)
+    right = [(i, (i + 1) % size) for i in range(size)]
+    tiles = [shard]
+    while len(tiles) < size:
+        tiles.append(lax.ppermute(tiles[-1], axis, right))
+    here = lax.axis_index(axis)
+    tiles = jnp.stack(tiles)[(here - jnp.arange(size)) % size]
+    return laid_out(tiles, dim)
 
 
 def passed_along(block, axis, distance):
@@ -69,7 +86,7 @@
     attn_set = (
         lax.all_gather(norm1_gain, "fsdp", axis=0, tiled=True),
         lax.all_gather(norm1_bias, "fsdp", axis=0, tiled=True),
-        lax.all_gather(qkv_weight, "fsdp", axis=0, tiled=True),
+        ring_gather(qkv_weight, "fsdp", 0),
         lax.all_gather(qv_bias, "fsdp", axis=0, tiled=True),
         lax.all_gather(out_weight, "fsdp", axis=0, tiled=True),
         lax.all_gather(out_bias, "fsdp", axis=0, tiled=True),

time: 1540 us -> 1520 us (0.987)
  waiting for transfers between devices: 1130 us -> 892 us
  blocking collectives: 135 us -> 302 us
  starting transfers between devices: 90.4 us -> 131 us
    all_gather x1, waiting for transfers between devices: 143 us -> 0.01 us  [shards(): lax.all_gather(down_weight, 'fsdp', axis=0, tiled=True)]
    all_gather x1, waiting for transfers between devices: 105 us -> 0.02 us  [shards(): lax.all_gather(up_weight, 'fsdp', axis=0, tiled=True)]
    all_gather x1, blocking collectives: 8.48 us -> 98.5 us  [shards(): lax.all_gather(norm1_bias, 'fsdp', axis=0, tiled=True)]
    all_gather x1, blocking collectives: 12.6 us -> 86.2 us  [shards(): lax.all_gather(out_bias, 'fsdp', axis=0, tiled=True)]
    ppermute x0 -> x3, waiting for transfers between devices: none -> 61.1 us  [ring_gather(): tiles.append(lax.ppermute(tiles[-1], axis, right))]
    all_gather x1 -> x0, waiting for transfers between devices: 34.6 us -> none  [shards(): lax.all_gather(qkv_weight, 'fsdp', axis=0, tiled=True)]
    ppermute x32, starting transfers between devices: 27.6 us -> 53.1 us  [from_behind(): return lax.ppermute(x, axis, [(i, (i + by) % size) for i in range(size)])]
    ppermute x32, waiting for transfers between devices: 50 us -> 31.4 us  [from_behind(): return lax.ppermute(x, axis, [(i, (i + by) % size) for i in range(size)])]
  transfers between devices with their start and end apart: 54 -> 56, of which waited for: 29 -> 26; matrix products, arithmetic and copies ran while one was open for 9% -> 10% of each run, Pallas kernels for 0% -> 0%
where the time goes in v1:
time: 1520 us
  waiting for transfers between devices  892 us (59%)
  blocking collectives  302 us (20%)
  starting transfers between devices  131 us (9%)
  matrix products  114 us (8%)
  other arithmetic  31.2 us (2%)
  local copies, waits for them, and re-layouts  30.6 us (2%)
    reduce_scatter x1, waiting for transfers between devices, shards(): lax.psum_scatter(up_w_grad, ('ctx', 'fsdp'), scatter_dimension=0, tiled=T...  366 us
    reduce_scatter x1, waiting for transfers between devices, shards(): lax.psum_scatter(down_w_grad, ('ctx', 'fsdp'), scatter_dimension=0, tiled...  365 us
    all_gather x1, blocking collectives, shards(): lax.all_gather(norm1_bias, 'fsdp', axis=0, tiled=True)  98.5 us
    all_gather x1, blocking collectives, shards(): lax.all_gather(out_bias, 'fsdp', axis=0, tiled=True)  86.2 us
    ppermute x14, starting transfers between devices, passed_along(): return lax.ppermute(block, axis, route)  64.7 us
    reduce_scatter x1, waiting for transfers between devices, shards(): lax.psum_scatter(qkv_w_grad, ('ctx', 'fsdp'), scatter_dimension=0, tiled=...  62.9 us
    ppermute x3, waiting for transfers between devices, ring_gather(): tiles.append(lax.ppermute(tiles[-1], axis, right))  61.1 us
    ppermute x32, starting transfers between devices, from_behind(): return lax.ppermute(x, axis, [(i, (i + by) % size) for i in range(size)])  53.1 us
  transfers between devices with their start and end apart: 56, of which 26 were waited for; matrix products, arithmetic and copies ran while one was open for 10% of the time, Pallas kernels for 0%

profile of v1, /device:TPU:0, one launch (start us, length us, event | category | flops | bytes accessed | tf_op | source)
XLA Modules:
  0.0 1517.0 jit_solution(3306820267182475700)
XLA Ops:
  11.9 61.1 %collective-permute-done.6 = bf16[256,3072]{1,0:T(8,128)(2,1)} collective-permute-done((bf16[256,3072]{1,0:T(8,128)(2,1)S(1)}, bf16[256,3072]{1,0:T(8,128)(2,1)}, u32[]{:S(2)}, u32[]{:S(2)}) %collective-permute-start.6) | collective-permute-done | bytes 1572896 | tf_op jit(solution)/shard_map/ppermute | solution.py:23
  73.0 7.8 collective-permute-start.7
  81.0 86.2 %all-gather.3 = bf16[4,1,256]{2,1,0:T(2,128)(2,1)S(1)} all-gather(bf16[1,1,256]{2,1,0:T(2,128)(2,1)S(1)} %reshape.473), channel_id=1, replica_groups=mesh['ctx'=8,'fsdp'=4] {'fsdp'}, dimensions={0}, use_global_device_ids=true | all-gather | bytes 2560 | tf_op jit(solution)/shard_map/all_gather | solution.py:92
  167.2 21.8 %all-gather.2 = bf16[4,1,512]{2,1,0:T(2,128)(2,1)S(1)} all-gather(bf16[1,1,512]{2,1,0:T(2,128)(2,1)S(1)} %reshape.471), channel_id=1, replica_groups=mesh['ctx'=8,'fsdp'=4] {'fsdp'}, dimensions={0}, use_global_device_ids=true | all-gather | bytes 5120 | tf_op jit(solution)/shard_map/all_gather | solution.py:90
  191.3 98.5 %all-gather.1 = bf16[4,1,256]{2,1,0:T(2,128)(2,1)S(1)} all-gather(bf16[1,1,256]{2,1,0:T(2,128)(2,1)S(1)} %reshape.469), channel_id=1, replica_groups=mesh['ctx'=8,'fsdp'=4] {'fsdp'}, dimensions={0}, use_global_device_ids=true | all-gather | bytes 2560 | tf_op jit(solution)/shard_map/all_gather | solution.py:88
  289.8 7.7 all-gather
  297.7 16.2 %all_gather.41 = bf16[4096]{0:T(1024)(128)(2,1)S(1)} all-gather(bf16[1024]{0:T(1024)(128)(2,1)S(1)} %copy-done.10), channel_id=1, replica_groups=mesh['ctx'=8,'fsdp'=4] {'fsdp'}, dimensions={0}, use_global_device_ids=true | all-gather | bytes 10240 | tf_op jit(solution)/shard_map/all_gather | solution.py:152
  313.9 7.7 all-gather.5
  321.7 10.7 all-gather.4
  333.1 6.6 pad_maximum_fusion
  339.6 6.4 gather_fusion
  354.7 81.5 %while.48 = (s32[]{:T(128)}, bf16[128,16,64]{0,2,1:T(8,128)(2,1)S(1)}, bf16[128,16,64]{0,2,1:T(8,128)(2,1)}, f32[128,16,64]{0,2,1:T(8,128)S(1)}, f32[16,128]{1,0...) while((s32[]{:T(128)}, ...), condition=%wide.region_10.11_spmd.clone, body=%wide.region_6.10_spmd.clone.sunk | while | flops 69264528 | bytes 8294802 | solution.py:139
  356.0 8.5 collective-permute-start.1
  444.9 7.8 convert_reduce_fusion.2
  462.5 152.0 %while.49 = (s32[]{:T(128)}, bf16[128,16,64]{0,2,1:T(8,128)(2,1)S(1)}, bf16[128,16,64]{0,2,1:T(8,128)(2,1)}, f32[128,16,64]{0,2,1:T(8,128)S(1)}, f32[128,16,64]{...) while((s32[]{:T(128)}, ...), condition=%wide.region_18.19_spmd.clone, body=%wide.region_16.18_spmd.clone.sunk | while | flops 171232400 | bytes 16044550 | solution.py:238
  615.7 6.4 fusion.62
  623.3 8.9 fusion.86
  633.2 10.7 fusion.64
  644.5 7.9 all-gather.6
  659.6 45.0 %all-reduce.8 = (f32[1024]{0:T(1024)S(1)}, f32[1024]{0:T(1024)S(1)}, f32[2048]{0:T(1024)S(1)}, f32[1024]{0:T(1024)S(1)}, f32[1024]{0:T(1024)S(1)}, /*index=5*/f3...) all-reduce(f32[1024]{0:T(1024)S(1)} %get-tuple-element.720, ...), channel_id=2, replica_groups=mesh['ctx'=8,'fsdp'=4] {'ctx','fsdp'}, use_global_device_ids=true, to_apply=%region_22.23.clone | all-reduce | flops 12288 | bytes 98304
  709.3 6.6 fusion.37
  715.8 62.9 %reduce-scatter.5.cloned.1.call-done = f32[32,3072]{1,0:T(8,128)} async-done(((f32[1024,3072]{1,0:T(8,128)}), f32[32,3072]{1,0:T(8,128)}) %reduce-scatter.5.cloned.1.call-update) | async-done | bytes 393232 | tf_op jit(solution)/shard_map/reduce_scatter | solution.py:262
  778.8 366.2 %reduce-scatter.9.cloned.1.call-done = f32[32,4096]{1,0:T(8,128)} async-done(((f32[1024,4096]{1,0:T(8,128)}), f32[32,4096]{1,0:T(8,128)}) %reduce-scatter.9.cloned.1.call-update) | async-done | bytes 524304 | tf_op jit(solution)/shard_map/reduce_scatter | solution.py:184
  1144.9 365.2 %reduce-scatter.11.cloned.1.call-done = f32[128,1024]{1,0:T(8,128)} async-done(((f32[4096,1024]{1,0:T(8,128)}), f32[128,1024]{1,0:T(8,128)}) %reduce-scatter.11.cloned.1.call-update) | async-done | bytes 524304 | tf_op jit(solution)/shard_map/reduce_scatter | solution.py:186
  (418 shorter events, 273.5 us)
Async XLA Ops:
  7.2 429.2 %all-gather.11.cloned.1.call-start = ((), (), s32[]{:S(2)}) async-start(), calls=%async_computation.4 | async-start | bytes 2621440 | tf_op jit(solution)/shard_map/all_gather | solution.py:91
  8.0 430.7 %all-gather.13.cloned.1.call-start = ((), (), s32[]{:S(2)}) async-start(), calls=%async_computation.5 | async-start | bytes 10485760 | tf_op jit(solution)/shard_map/all_gather | solution.py:151
  8.8 436.1 %all-gather.15.cloned.1.call-start = ((), (), s32[]{:S(2)}) async-start(), calls=%async_computation.6 | async-start | bytes 10485760 | tf_op jit(solution)/shard_map/all_gather | solution.py:153
  8.8 64.2 %collective-permute-start.6 = (bf16[256,3072]{1,0:T(8,128)(2,1)S(1)}, bf16[256,3072]{1,0:T(8,128)(2,1)}, u32[]{:S(2)}, u32[]{:S(2)}) collective-permute-start(bf16[256,3072]{1,0:T(8,128)(2,1)S(1)} %copy-done.9), channel_id=1, source_target_pairs={{0,1},{1,2},{2,3},{3,0},{4,5},{5,6},{6,7},{7,4},{8,9},{9,10},{10,1... | collective-permute-start | bytes 4718600 | tf_op jit(solution)/shard_map/ppermute | solution.py:23
  73.0 116.0 %collective-permute-start.7 = (bf16[256,3072]{1,0:T(8,128)(2,1)}, bf16[256,3072]{1,0:T(8,128)(2,1)}, u32[]{:S(2)}, u32[]{:S(2)}) collective-permute-start(bf16[256,3072]{1,0:T(8,128)(2,1)} %collective-permute-done.6), channel_id=1, source_target_pairs={{0,1},{1,2},{2,3},{3,0},{4,5},{5,6},{6,7},{7,4},{8,9},{9,10},{10,1... | collective-permute-start | bytes 4718600 | tf_op jit(solution)/shard_map/ppermute | solution.py:23
  80.9 635.0 %reduce-scatter.7.cloned.1.call-start = ((), (), s32[]{:S(2)}) async-start(), calls=%async_computation.8 | async-start | bytes 4325376 | tf_op jit(solution)/shard_map/reduce_scatter | solution.py:264
  189.0 144.1 %collective-permute-start.8 = (bf16[256,3072]{1,0:T(8,128)(2,1)}, bf16[256,3072]{1,0:T(8,128)(2,1)}, u32[]{:S(2)}, u32[]{:S(2)}) collective-permute-start(bf16[256,3072]{1,0:T(8,128)(2,1)} %collective-permute-done.7), channel_id=1, source_target_pairs={{0,1},{1,2},{2,3},{3,0},{4,5},{5,6},{6,7},{7,4},{8,9},{9,10},{10,1... | collective-permute-start | bytes 4718600 | tf_op jit(solution)/shard_map/ppermute | solution.py:23
  462.4 316.3 %reduce-scatter.5.cloned.1.call-start = ((), (), s32[]{:S(2)}) async-start(), calls=%async_computation.7 | async-start | bytes 12976128 | tf_op jit(solution)/shard_map/reduce_scatter | solution.py:262
  462.8 20.4 %collective-permute-start.2 = (bf16[128,16,64]{0,2,1:T(8,128)(2,1)S(1)}, bf16[128,16,64]{0,2,1:T(8,128)(2,1)S(1)}, u32[]{:S(2)}, u32[]{:S(2)}) collective-permute-start(bf16[128,16,64]{0,2,1:T(8,128)(2,1)S(1)} %copy.89), channel_id=1, source_target_pairs={{0,4},{4,8},{8,12},{12,16},{16,20},{20,24},{24,28},{28,0},{1,5},{5... | collective-permute-start | bytes 786440 | tf_op jit(solution)/shard_map/while/body/eval_jaxpr/ppermute | solution.py:37
  483.2 20.0 %collective-permute-start.2 = (bf16[128,16,64]{0,2,1:T(8,128)(2,1)S(1)}, bf16[128,16,64]{0,2,1:T(8,128)(2,1)S(1)}, u32[]{:S(2)}, u32[]{:S(2)}) collective-permute-start(bf16[128,16,64]{0,2,1:T(8,128)(2,1)S(1)} %copy.89), channel_id=1, source_target_pairs={{0,4},{4,8},{8,12},{12,16},{16,20},{20,24},{24,28},{28,0},{1,5},{5... | collective-permute-start | bytes 786440 | tf_op jit(solution)/shard_map/while/body/eval_jaxpr/ppermute | solution.py:37
  503.2 18.7 %collective-permute-start.2 = (bf16[128,16,64]{0,2,1:T(8,128)(2,1)S(1)}, bf16[128,16,64]{0,2,1:T(8,128)(2,1)S(1)}, u32[]{:S(2)}, u32[]{:S(2)}) collective-permute-start(bf16[128,16,64]{0,2,1:T(8,128)(2,1)S(1)} %copy.89), channel_id=1, source_target_pairs={{0,4},{4,8},{8,12},{12,16},{16,20},{20,24},{24,28},{28,0},{1,5},{5... | collective-permute-start | bytes 786440 | tf_op jit(solution)/shard_map/while/body/eval_jaxpr/ppermute | solution.py:37
  504.3 17.7 %collective-permute-start.3 = (bf16[128,16,64]{0,2,1:T(8,128)(2,1)S(1)}, bf16[128,16,64]{0,2,1:T(8,128)(2,1)}, u32[]{:S(2)}, u32[]{:S(2)}) collective-permute-start(bf16[128,16,64]{0,2,1:T(8,128)(2,1)S(1)} %copy.90), channel_id=1, source_target_pairs={{0,4},{4,8},{8,12},{12,16},{16,20},{20,24},{24,28},{28,0},{1,5},{5... | collective-permute-start | bytes 786440 | tf_op jit(solution)/shard_map/while/body/eval_jaxpr/ppermute | solution.py:37
  522.0 18.6 %collective-permute-start.2 = (bf16[128,16,64]{0,2,1:T(8,128)(2,1)S(1)}, bf16[128,16,64]{0,2,1:T(8,128)(2,1)S(1)}, u32[]{:S(2)}, u32[]{:S(2)}) collective-permute-start(bf16[128,16,64]{0,2,1:T(8,128)(2,1)S(1)} %copy.89), channel_id=1, source_target_pairs={{0,4},{4,8},{8,12},{12,16},{16,20},{20,24},{24,28},{28,0},{1,5},{5... | collective-permute-start | bytes 786440 | tf_op jit(solution)/shard_map/while/body/eval_jaxpr/ppermute | solution.py:37
  523.1 17.5 %collective-permute-start.3 = (bf16[128,16,64]{0,2,1:T(8,128)(2,1)S(1)}, bf16[128,16,64]{0,2,1:T(8,128)(2,1)}, u32[]{:S(2)}, u32[]{:S(2)}) collective-permute-start(bf16[128,16,64]{0,2,1:T(8,128)(2,1)S(1)} %copy.90), channel_id=1, source_target_pairs={{0,4},{4,8},{8,12},{12,16},{16,20},{20,24},{24,28},{28,0},{1,5},{5... | collective-permute-start | bytes 786440 | tf_op jit(solution)/shard_map/while/body/eval_jaxpr/ppermute | solution.py:37
  540.6 18.4 %collective-permute-start.2 = (bf16[128,16,64]{0,2,1:T(8,128)(2,1)S(1)}, bf16[128,16,64]{0,2,1:T(8,128)(2,1)S(1)}, u32[]{:S(2)}, u32[]{:S(2)}) collective-permute-start(bf16[128,16,64]{0,2,1:T(8,128)(2,1)S(1)} %copy.89), channel_id=1, source_target_pairs={{0,4},{4,8},{8,12},{12,16},{16,20},{20,24},{24,28},{28,0},{1,5},{5... | collective-permute-start | bytes 786440 | tf_op jit(solution)/shard_map/while/body/eval_jaxpr/ppermute | solution.py:37
  541.7 17.4 %collective-permute-start.3 = (bf16[128,16,64]{0,2,1:T(8,128)(2,1)S(1)}, bf16[128,16,64]{0,2,1:T(8,128)(2,1)}, u32[]{:S(2)}, u32[]{:S(2)}) collective-permute-start(bf16[128,16,64]{0,2,1:T(8,128)(2,1)S(1)} %copy.90), channel_id=1, source_target_pairs={{0,4},{4,8},{8,12},{12,16},{16,20},{20,24},{24,28},{28,0},{1,5},{5... | collective-permute-start | bytes 786440 | tf_op jit(solution)/shard_map/while/body/eval_jaxpr/ppermute | solution.py:37
  559.1 18.4 %collective-permute-start.2 = (bf16[128,16,64]{0,2,1:T(8,128)(2,1)S(1)}, bf16[128,16,64]{0,2,1:T(8,128)(2,1)S(1)}, u32[]{:S(2)}, u32[]{:S(2)}) collective-permute-start(bf16[128,16,64]{0,2,1:T(8,128)(2,1)S(1)} %copy.89), channel_id=1, source_target_pairs={{0,4},{4,8},{8,12},{12,16},{16,20},{20,24},{24,28},{28,0},{1,5},{5... | collective-permute-start | bytes 786440 | tf_op jit(solution)/shard_map/while/body/eval_jaxpr/ppermute | solution.py:37
  560.2 17.4 %collective-permute-start.3 = (bf16[128,16,64]{0,2,1:T(8,128)(2,1)S(1)}, bf16[128,16,64]{0,2,1:T(8,128)(2,1)}, u32[]{:S(2)}, u32[]{:S(2)}) collective-permute-start(bf16[128,16,64]{0,2,1:T(8,128)(2,1)S(1)} %copy.90), channel_id=1, source_target_pairs={{0,4},{4,8},{8,12},{12,16},{16,20},{20,24},{24,28},{28,0},{1,5},{5... | collective-permute-start | bytes 786440 | tf_op jit(solution)/shard_map/while/body/eval_jaxpr/ppermute | solution.py:37
  577.6 18.4 %collective-permute-start.2 = (bf16[128,16,64]{0,2,1:T(8,128)(2,1)S(1)}, bf16[128,16,64]{0,2,1:T(8,128)(2,1)S(1)}, u32[]{:S(2)}, u32[]{:S(2)}) collective-permute-start(bf16[128,16,64]{0,2,1:T(8,128)(2,1)S(1)} %copy.89), channel_id=1, source_target_pairs={{0,4},{4,8},{8,12},{12,16},{16,20},{20,24},{24,28},{28,0},{1,5},{5... | collective-permute-start | bytes 786440 | tf_op jit(solution)/shard_map/while/body/eval_jaxpr/ppermute | solution.py:37
  578.6 17.4 %collective-permute-start.3 = (bf16[128,16,64]{0,2,1:T(8,128)(2,1)S(1)}, bf16[128,16,64]{0,2,1:T(8,128)(2,1)}, u32[]{:S(2)}, u32[]{:S(2)}) collective-permute-start(bf16[128,16,64]{0,2,1:T(8,128)(2,1)S(1)} %copy.90), channel_id=1, source_target_pairs={{0,4},{4,8},{8,12},{12,16},{16,20},{20,24},{24,28},{28,0},{1,5},{5... | collective-permute-start | bytes 786440 | tf_op jit(solution)/shard_map/while/body/eval_jaxpr/ppermute | solution.py:37
  596.0 18.4 %collective-permute-start.2 = (bf16[128,16,64]{0,2,1:T(8,128)(2,1)S(1)}, bf16[128,16,64]{0,2,1:T(8,128)(2,1)S(1)}, u32[]{:S(2)}, u32[]{:S(2)}) collective-permute-start(bf16[128,16,64]{0,2,1:T(8,128)(2,1)S(1)} %copy.89), channel_id=1, source_target_pairs={{0,4},{4,8},{8,12},{12,16},{16,20},{20,24},{24,28},{28,0},{1,5},{5... | collective-permute-start | bytes 786440 | tf_op jit(solution)/shard_map/while/body/eval_jaxpr/ppermute | solution.py:37
  597.1 17.4 %collective-permute-start.3 = (bf16[128,16,64]{0,2,1:T(8,128)(2,1)S(1)}, bf16[128,16,64]{0,2,1:T(8,128)(2,1)}, u32[]{:S(2)}, u32[]{:S(2)}) collective-permute-start(bf16[128,16,64]{0,2,1:T(8,128)(2,1)S(1)} %copy.90), channel_id=1, source_target_pairs={{0,4},{4,8},{8,12},{12,16},{16,20},{20,24},{24,28},{28,0},{1,5},{5... | collective-permute-start | bytes 786440 | tf_op jit(solution)/shard_map/while/body/eval_jaxpr/ppermute | solution.py:37
  622.1 522.8 %reduce-scatter.9.cloned.1.call-start = ((), (), s32[]{:S(2)}) async-start(), calls=%async_computation.9 | async-start | bytes 17301504 | tf_op jit(solution)/shard_map/reduce_scatter | solution.py:184
  632.2 877.9 %reduce-scatter.11.cloned.1.call-start = ((), (), s32[]{:S(2)}) async-start(), calls=%async_computation.10 | async-start | bytes 17301504 | tf_op jit(solution)/shard_map/reduce_scatter | solution.py:186
  (51 other events, 2544.5 us)
Sparse Core Ops, SparseCore 0:
  9.6 72.8 all-gather.10
  84.1 202.8 all-gather.12
  288.5 148.8 all-gather.14
  462.6 154.8 reduce-scatter.6
  623.9 154.7 reduce-scatter.4
  781.6 363.3 reduce-scatter.8
  1147.9 362.1 reduce-scatter.10
